TPU v7x, 256 devices: a whole 4x4x8 slice. The times are simulated.
256 devices in a mesh: seq: 64 (over y, z, core), tp: 4 (over x).
Axes of the slice: x: 4, y: 4, z: 8, core: 2. Of those that a mesh axis runs over, the one named last changes fastest.
Arguments:
- queries_short: bfloat16 [128, 4, 2304], P('seq', None, 'tp'), may hold values from -4 to 4
- cache_short: bfloat16 [2, 128, 1024, 2304], P(None, 'seq', None, 'tp'), may hold values from -260 to 260
- fresh_short: bfloat16 [2, 128, 4, 2304], P(None, 'seq', None, 'tp'), may hold values from -260 to 260
- short_len: int32 [128], P('seq'), may hold values from 1 to 1024, as said below
- queries_long: bfloat16 [4, 4, 2304], P(None, None, 'tp'), may hold values from -4 to 4
- cache_long: bfloat16 [2, 4, 16384, 2304], P(None, None, 'seq', 'tp'), may hold values from -260 to 260
- fresh_long: bfloat16 [2, 4, 4, 2304], P(None, None, None, 'tp'), may hold values from -260 to 260
- long_len: int32 [4], replicated, may hold values from 8192 to 16384, as said below
- block_live: int32 [4, 128], P(None, 'seq'), may hold values 0 or 1
- out_weight: bfloat16 [2304, 2304], P('tp'), may hold values from -0.125 to 0.125
Outputs:
- short_out: bfloat16 [128, 4, 2304], P('seq', None, 'tp')
- long_out: bfloat16 [4, 4, 2304], P(None, None, 'tp')
Inputs may be any that keep to these rules, and one draw needn't show every extreme that they name: `short_len`: some short request fills all 1024 slots. `long_len`: some long request fills all 16384 slots.
All inputs are finite; a program needn't handle non-finite values. No bound on the sum of `block_live` on one device may be relied on, other than what follows from the above.
Results may differ from a plain program's by a relative error of at most 0.011.
Values sent between devices are 32-bit elements; how exact they have to be, the bound alone decides.
A program may use at most 64 MiB of HBM per device.

v0:
```python
import math
import jax
import jax.numpy as jnp
from jax import lax
from jax.sharding import PartitionSpec as P

HEAD_DIM = 64
NEGATIVE = -1e30


def split_heads(tensor):
    return tensor.reshape(tensor.shape[0], tensor.shape[1], tensor.shape[2] // HEAD_DIM, HEAD_DIM)


def partial_softmax(query_heads, key_heads, value_heads, usable):
    scores = jnp.einsum(
        "rjhd,rphd->rhjp", query_heads, key_heads, preferred_element_type=jnp.float32
    ) * (1.0 / math.sqrt(HEAD_DIM))
    scores = jnp.where(usable, scores, NEGATIVE)
    highest = jnp.max(scores, axis=-1)
    expo = jnp.where(usable, jnp.exp(scores - highest[..., None]), 0.0)
    totals = jnp.sum(expo, axis=-1)
    summed = jnp.einsum(
        "rhjp,rphd->rhjd",
        expo.astype(jnp.bfloat16),
        value_heads,
        preferred_element_type=jnp.float32,
    )
    return (highest, totals, summed)


def combine_parts(first, second):
    highest = jnp.maximum(first[0], second[0])
    scale_first = jnp.exp(first[0] - highest)
    scale_second = jnp.exp(second[0] - highest)
    totals = first[1] * scale_first + second[1] * scale_second
    summed = first[2] * scale_first[..., None] + second[2] * scale_second[..., None]
    return (highest, totals, summed)


def finish(parts):
    normed = (parts[2] / parts[1][..., None]).astype(jnp.bfloat16)
    normed = jnp.transpose(normed, (0, 2, 1, 3))
    return normed.reshape(normed.shape[0], normed.shape[1], normed.shape[2] * normed.shape[3])


def fresh_part(queries, fresh):
    count = queries.shape[1]
    causal = (jnp.arange(count)[:, None] >= jnp.arange(count)[None, :])[None, None]
    return partial_softmax(
        split_heads(queries), split_heads(fresh[0]), split_heads(fresh[1]), causal
    )


def per_device(
    queries_short,
    cache_short,
    fresh_short,
    short_len,
    queries_long,
    cache_long,
    fresh_long,
    long_len,
    block_live,
    out_weight,
):
    short_query = split_heads(queries_short)
    request_count = queries_short.shape[0]
    token_count = queries_short.shape[1]
    positions = cache_short.shape[2]
    usable = (jnp.arange(positions, dtype=jnp.int32)[None, :] < short_len[:, None])[
        :, None, None, :
    ]
    short_parts = partial_softmax(
        short_query, split_heads(cache_short[0]), split_heads(cache_short[1]), usable
    )
    short_att = finish(combine_parts(short_parts, fresh_part(queries_short, fresh_short)))
    local_len = cache_long.shape[2]
    spots = lax.axis_index("seq") * local_len + jnp.arange(local_len, dtype=jnp.int32)
    live = jnp.repeat(block_live, local_len // block_live.shape[1], axis=1) == 1
    long_usable = ((spots[None, :] < long_len[:, None]) & live)[:, None, None, :]
    long_parts = partial_softmax(
        split_heads(queries_long),
        split_heads(cache_long[0]),
        split_heads(cache_long[1]),
        long_usable,
    )
    every_high, every_total, every_sum = (
        lax.all_gather(long_parts[0][None], "seq", axis=0, tiled=True),
        lax.all_gather(long_parts[1][None], "seq", axis=0, tiled=True),
        lax.all_gather(long_parts[2][None], "seq", axis=0, tiled=True),
    )
    highest = jnp.max(every_high, axis=0)
    scales = jnp.exp(every_high - highest[None])
    merged = (
        highest,
        jnp.sum(every_total * scales, axis=0),
        jnp.sum(every_sum * scales[..., None], axis=0),
    )
    long_att = finish(combine_parts(merged, fresh_part(queries_long, fresh_long)))
    short_term = jnp.dot(
        short_att.reshape(-1, short_att.shape[2]), out_weight, preferred_element_type=jnp.float32
    )
    long_term = jnp.dot(
        long_att.reshape(-1, long_att.shape[2]), out_weight, preferred_element_type=jnp.float32
    )
    short_cols = lax.psum_scatter(short_term, "tp", scatter_dimension=1, tiled=True)
    long_cols = lax.psum_scatter(long_term, "tp", scatter_dimension=1, tiled=True)
    short_out = short_cols.astype(jnp.bfloat16).reshape(
        request_count, token_count, short_cols.shape[1]
    )
    long_out = long_cols.astype(jnp.bfloat16).reshape(
        long_att.shape[0], long_att.shape[1], long_cols.shape[1]
    )
    return (short_out, long_out)


def solution(mesh):
    in_specs = (
        P("seq", None, "tp"),
        P(None, "seq", None, "tp"),
        P(None, "seq", None, "tp"),
        P("seq"),
        P(None, None, "tp"),
        P(None, None, "seq", "tp"),
        P(None, None, None, "tp"),
        P(),
        P(None, "seq"),
        P("tp", None),
    )
    out_specs = (P("seq", None, "tp"), P(None, None, "tp"))
    return jax.shard_map(
        per_device, mesh=mesh, in_specs=in_specs, out_specs=out_specs, check_vma=False
    )
```

profile of v0, /device:TPU:8, one launch (start us, length us, event | category | flops | bytes accessed | tf_op | source)
XLA Modules:
  0.0 182.1 jit_solution(8602789161538166098)
XLA Ops:
  8.1 0.8 broadcast_compare_fusion
  8.9 3.2 %fusion.53 = (bf16[1,4,256,576]{2,3,1,0:T(8,128)(2,1)}, bf16[1,4,256,576]{2,3,1,0:T(8,128)(2,1)}) fusion(bf16[2,4,256,576]{2,3,1,0:T(8,128)(2,1)} %param.15), kind=kLoop, calls=%fused_computation.77 | loop fusion | bytes 4718592 | tf_op jit(solution)/shard_map/slice | solution.py:84
  12.2 0.1 reshape.139
  12.3 1.6 fusion.57
  14.0 2.4 %fusion.19 = f32[4,9,4,64]{3,2,1,0:T(4,128)} fusion(bf16[4,256,9,64]{1,3,2,0:T(8,128)(2,1)} %bitcast.96, f32[4,9,4,256]{3,2,1,0:T(4,128)S(1)} %get-tuple-element.23, f32[4,9,4]{2,1,0:T(8,128)S(1)} %get-tuple-element.22, pred[4,256]{1,0:T(4,128)(4,1)S(1)} %bitcast_and_fusion), kind=kOutput, calls=%fused_computation.30 | convolution fusion | flops 4829184 | bytes 1365568 | tf_op jit(solution)/shard_map/rhjp,rphd->rhjd/dot_general | solution.py:23
  16.6 0.1 fusion.29
  16.8 0.1 copy.143
  16.9 0.1 fusion.36
  17.0 0.1 copy.144
  17.1 0.1 fusion.45
  17.2 0.1 copy.147
  17.3 0.1 copy.145
  17.6 2.9 %fusion.52 = (bf16[1,2,1024,576]{2,3,1,0:T(8,128)(2,1)S(1)}, bf16[1,2,1024,576]{2,3,1,0:T(8,128)(2,1)S(1)}) fusion(bf16[2,2,1024,576]{2,3,1,0:T(8,128)(2,1)} %param.11), kind=kLoop, calls=%fused_computation.76 | loop fusion | bytes 9437184 | tf_op jit(solution)/shard_map/slice | solution.py:75
  20.5 0.5 fusion.56
  21.0 0.3 fusion.11
  21.3 0.7 fusion.9
  22.1 0.2 fusion.10
  22.3 0.1 reshape_reshape.6
  22.4 2.2 %convolution_bitcast_fusion.1 = f32[2304,8]{1,0:T(8,128)} fusion(bf16[8,576]{1,0:T(8,128)(2,1)S(1)} %reshape_reshape.6, bf16[576,2304]{1,0:T(8,128)(2,1)S(1)} %copy-done), kind=kOutput, calls=%fused_computation.2 | convolution fusion | flops 21233664 | bytes 2737152
  24.7 0.1 copy.150
  24.8 0.2 fusion.17
  25.0 53.0 %all-gather.1 = f32[256,9,4]{1,2,0:T(4,128)S(1)} all-gather(f32[4,9,4]{1,2,0:T(4,128)S(1)} %copy.150), channel_id=3, replica_groups=mesh['seq'=64,'tp'=4] {'seq'}, dimensions={0}, use_global_device_ids=true | all-gather | bytes 37440 | tf_op jit(solution)/shard_map/all_gather | solution.py:89
  78.0 0.8 copy-done.1
  78.8 0.1 reduce_max.58
  79.0 1.2 subtract_exponential_fusion
  80.2 0.1 copy.162
  80.3 52.9 %all-gather.2 = f32[256,9,4]{1,2,0:T(4,128)} all-gather(f32[4,9,4]{1,2,0:T(4,128)S(1)} %copy.162), channel_id=4, replica_groups=mesh['seq'=64,'tp'=4] {'seq'}, dimensions={0}, use_global_device_ids=true | all-gather | bytes 37440 | tf_op jit(solution)/shard_map/all_gather | solution.py:90
  133.2 3.0 %copy.151 = f32[64,4,9,4]{3,2,1,0:T(8,128)} copy(f32[64,4,9,4]{2,3,1,0:T(4,128)S(1)} %subtract_exponential_fusion) | data formatting | bytes 73728 | tf_op jit(solution)/shard_map/exp | solution.py:94
  136.2 1.2 multiply_reduce_fusion.1
  137.5 0.1 reshape_squeeze.30
  137.6 0.2 fusion.25
  137.7 0.2 copy.154
  137.9 0.1 fusion.27
  138.1 0.1 fusion.37
  138.2 0.1 copy.157
  138.3 0.1 copy.161
  138.4 0.1 copy.165
  138.5 0.2 copy.159
  138.8 0.1 reshape_squeeze.31
  138.9 6.3 %multiply_reduce_fusion = f32[4,9,4,64]{3,2,1,0:T(4,128)S(1)} fusion(f32[64,4,9,4,64]{4,3,2,1,0:T(4,128)} %bitcast.91, f32[64,4,9,4]{3,2,1,0:T(8,128)} %copy.151), kind=kLoop, calls=%fused_computation | loop fusion | flops 1170432 | bytes 2433024 | tf_op jit(solution)/shard_map/reduce_sum | solution.py:98
  145.2 0.2 fusion.5
  145.4 0.1 reshape_reshape.7
  145.5 2.2 %convolution_bitcast_fusion = f32[2304,16]{1,0:T(8,128)} fusion(bf16[16,576]{1,0:T(8,128)(2,1)S(1)} %reshape_reshape.7, bf16[576,2304]{1,0:T(8,128)(2,1)S(1)} %copy-done), kind=kOutput, calls=%fused_computation.1 | convolution fusion | flops 42467328 | bytes 2820096
  147.7 1.0 copy.168
  148.8 0.6 reshape.138
  149.4 23.5 %reduce-scatter.9.cloned.1.call-done = f32[576,16]{1,0:T(8,128)} async-done(((f32[2304,16]{1,0:T(8,128)}), f32[576,16]{1,0:T(8,128)}) %reduce-scatter.9.cloned.1.call-update) | async-done | bytes 36880
  172.9 1.1 copy.170
  174.0 0.6 reshape.140
  (36 shorter events, 0.8 us)
Async XLA Ops:
  8.0 14.4 %copy-start = (bf16[576,2304]{1,0:T(8,128)(2,1)S(1)}, bf16[576,2304]{1,0:T(8,128)(2,1)}, u32[]{:S(2)}) copy-start(bf16[576,2304]{1,0:T(8,128)(2,1)} %param.19) | copy-start | bytes 7962628
  8.0 130.9 %all-gather.5.cloned.1.call-start = ((), (), s32[]{:S(2)}) async-start(), calls=%async_computation.2 | async-start | bytes 4792320 | tf_op jit(solution)/shard_map/all_gather | solution.py:91
  8.9 3.2 %copy-start.4 = (bf16[4,4,576]{2,1,0:T(4,128)(2,1)S(1)}, bf16[4,4,576]{2,1,0:T(4,128)(2,1)}, u32[]{:S(2)}) copy-start(bf16[4,4,576]{2,1,0:T(4,128)(2,1)} %param.14) | copy-start | bytes 55300
  8.9 3.4 %copy-start.7 = (s32[4]{0:T(128)S(1)}, s32[4]{0:T(128)}, u32[]{:S(2)}) copy-start(s32[4]{0:T(128)} %param.17) | copy-start | bytes 52
  12.1 4.3 %copy-start.5 = (bf16[2,4,576]{2,1,0:T(4,128)(2,1)S(1)}, bf16[2,4,576]{2,1,0:T(4,128)(2,1)}, u32[]{:S(2)}) copy-start(bf16[2,4,576]{2,1,0:T(4,128)(2,1)} %param.10) | copy-start | bytes 27652
  12.1 4.4 %copy-start.3 = (bf16[2,2,4,576]{3,2,1,0:T(4,128)(2,1)S(1)}, bf16[2,2,4,576]{3,2,1,0:T(4,128)(2,1)}, u32[]{:S(2)}) copy-start(bf16[2,2,4,576]{3,2,1,0:T(4,128)(2,1)} %param.12) | copy-start | bytes 55300
  12.1 5.4 %copy-start.6 = (s32[2]{0:T(128)S(1)}, s32[2]{0:T(128)}, u32[]{:S(2)}) copy-start(s32[2]{0:T(128)} %param.13) | copy-start | bytes 28
  16.4 131.4 %reduce-scatter.7.cloned.1.call-start = ((), (), s32[]{:S(2)}) async-start(), calls=%async_computation.3 | async-start | bytes 1474560
  24.6 148.3 %reduce-scatter.9.cloned.1.call-start = ((), (), s32[]{:S(2)}) async-start(), calls=%async_computation.4 | async-start | bytes 1474560
  78.0 0.8 copy-start.1
  80.2 57.3 %copy-start.2 = (bf16[2,4,4,576]{3,2,1,0:T(4,128)(2,1)S(1)}, bf16[2,4,4,576]{3,2,1,0:T(4,128)(2,1)}, u32[]{:S(2)}) copy-start(bf16[2,4,4,576]{3,2,1,0:T(4,128)(2,1)} %param.16) | copy-start | bytes 110596
Sparse Core Ops, SparseCore 0:
  16.5 81.3 all-gather.4
Sparse Core Ops, SparseCore 1:
  24.7 29.4 reduce-scatter.6
  147.8 25.1 reduce-scatter.8
where the time goes:
time: 183 us; the launch traced here: 182 us
  blocking collectives  106 us (58%)
  waiting for transfers between devices  23.6 us (13%)
  local copies, waits for them, and re-layouts  15.7 us (9%)
  between operations  15.7 us (9%)
  other arithmetic  10.8 us (6%)
  matrix products  10.3 us (6%)
    all_gather x1, blocking collectives, per_device(): lax.all_gather(long_parts[0][None], 'seq', axis=0, tiled=True)  53 us
    all_gather x1, blocking collectives, per_device(): lax.all_gather(long_parts[1][None], 'seq', axis=0, tiled=True)  52.9 us
    unnamed x5, waiting for transfers between devices  23.6 us
    reduce_sum x1, other arithmetic, per_device(): jnp.sum(every_sum * scales[..., None], axis=0)  6.27 us
    unnamed x2, matrix products  4.36 us
  transfers between devices with their start and end apart: 3, of which 1 were waited for; matrix products, arithmetic and copies ran while one was open for 14% of the time, Pallas kernels for 0%

commit v1 on v0

--- a/solution.py
+++ b/solution.py
@@ -6,6 +6,11 @@
 
 HEAD_DIM = 64
 NEGATIVE = -1e30
+
+
+def gather_over(value, name, along):
+    repeated = jnp.stack([value] * lax.axis_size(name))
+    return jnp.concatenate(lax.all_to_all(repeated, name, 0, 0), axis=along)
 
 
 def split_heads(tensor):
@@ -87,7 +92,7 @@
     )
     every_high, every_total, every_sum = (
         lax.all_gather(long_parts[0][None], "seq", axis=0, tiled=True),
-        lax.all_gather(long_parts[1][None], "seq", axis=0, tiled=True),
+        gather_over(long_parts[1][None], "seq", 0),
         lax.all_gather(long_parts[2][None], "seq", axis=0, tiled=True),
     )
     highest = jnp.max(every_high, axis=0)

time: 183 us -> 144 us (0.79)
  blocking collectives: 106 us -> 50.1 us
  starting transfers between devices: 0.13 us -> 12.2 us
  local copies, waits for them, and re-layouts: 15.7 us -> 19.1 us
    all_gather x1 -> x0, blocking collectives: 52.9 us -> none  [per_device(): lax.all_gather(long_parts[1][None], 'seq', axis=0, tiled=True)]
    all_to_all x0 -> x1, starting transfers between devices: none -> 12.1 us  [gather_over(): return jnp.concatenate(lax.all_to_all(repeated, name, 0, 0), axis=along)]
    all_gather x1, blocking collectives: 53 us -> 50.1 us  [per_device(): lax.all_gather(long_parts[0][None], 'seq', axis=0, tiled=True)]
    unnamed x18 -> x21, local copies, waits for them, and re-layouts: 2.96 us -> 5.79 us
  transfers between devices with their start and end apart: 3 -> 4, of which waited for: 1 -> 1; matrix products, arithmetic and copies ran while one was open for 14% -> 21% of each run, Pallas kernels for 0% -> 0%
where the time goes in v1:
time: 144 us; the launch traced here: 143 us
  blocking collectives  50.1 us (35%)
  waiting for transfers between devices  24.4 us (17%)
  local copies, waits for them, and re-layouts  19.1 us (13%)
  between operations  15.7 us (11%)
  starting transfers between devices  12.2 us (8%)
  other arithmetic  11.6 us (8%)
  matrix products  10.3 us (7%)
    all_gather x1, blocking collectives, per_device(): lax.all_gather(long_parts[0][None], 'seq', axis=0, tiled=True)  50.1 us
    unnamed x5, waiting for transfers between devices  24.4 us
    all_to_all x1, starting transfers between devices, gather_over(): return jnp.concatenate(lax.all_to_all(repeated, name, 0, 0), axis=along)  12.1 us
    reduce_sum x1, other arithmetic, per_device(): jnp.sum(every_sum * scales[..., None], axis=0)  6.27 us
    unnamed x21, local copies, waits for them, and re-layouts  5.79 us
    unnamed x2, matrix products  4.36 us
    dot_general x4, matrix products, partial_softmax(): jnp.einsum('rhjp,rphd->rhjd', expo.astype(jnp.bfloat16), value_heads, pre...  3.52 us
    slice x1, local copies, waits for them, and re-layouts, per_device(): cache_long[0]  3.22 us
  transfers between devices with their start and end apart: 4, of which 1 were waited for; matrix products, arithmetic and copies ran while one was open for 21% of the time, Pallas kernels for 0%

profile of v1, /device:TPU:8, one launch (start us, length us, event | category | flops | bytes accessed | tf_op | source)
XLA Modules:
  0.0 143.3 jit_solution(17467548271861947453)
XLA Ops:
  8.1 0.8 broadcast_compare_fusion
  8.9 3.2 %fusion.54 = (bf16[1,4,256,576]{2,3,1,0:T(8,128)(2,1)}, bf16[1,4,256,576]{2,3,1,0:T(8,128)(2,1)}) fusion(bf16[2,4,256,576]{2,3,1,0:T(8,128)(2,1)} %param.15), kind=kLoop, calls=%fused_computation.78 | loop fusion | bytes 4718592 | tf_op jit(solution)/shard_map/slice | solution.py:89
  12.3 1.6 %fusion.58 = (f32[4,9,4]{2,1,0:T(8,128)S(1)}, f32[4,9,4,256]{3,2,1,0:T(4,128)S(1)}) fusion(bf16[4,256,9,64]{1,3,2,0:T(8,128)(2,1)} %bitcast.100, bf16[4,4,9,64]{3,2,1,0:T(8,128)(2,1)S(1)} %reshape.144, pred[4,256]{1,0:T(4,128)(4,1)S(1)} %bitcast_and_fusion), kind=kOutput, calls=%fused_computation.82 | convolution fusion | flops 4829040 | bytes 1347136 | tf_op jit(solution)/shard_map/rjhd,rphd->rhjp/dot_general | solution.py:21
  14.0 2.4 %fusion.20 = f32[4,9,4,64]{3,2,1,0:T(4,128)} fusion(bf16[4,256,9,64]{1,3,2,0:T(8,128)(2,1)} %bitcast.102, f32[4,9,4,256]{3,2,1,0:T(4,128)S(1)} %get-tuple-element.23, f32[4,9,4]{2,1,0:T(8,128)S(1)} %get-tuple-element.22, pred[4,256]{1,0:T(4,128)(4,1)S(1)} %bitcast_and_fusion), kind=kOutput, calls=%fused_computation.31 | convolution fusion | flops 4829184 | bytes 1365568 | tf_op jit(solution)/shard_map/rhjp,rphd->rhjd/dot_general | solution.py:28
  16.4 0.2 fusion.18
  16.6 0.1 copy.162
  16.8 1.3 reshape.153
  18.0 12.1 %all-to-all-start = ((f32[64,1,144]{2,1,0:T(1,128)}), f32[64,1,144]{2,1,0:T(1,128)S(1)}, u32[]{:S(2)}, u32[]{:S(2)}) async-start(f32[64,1,144]{2,1,0:T(1,128)} %reshape.153), calls=%async_computation | async-start | bytes 131072 | tf_op jit(solution)/shard_map/all_to_all | solution.py:13
  30.4 0.1 fusion.30
  30.5 0.1 copy.143
  30.7 0.1 fusion.37
  30.8 0.1 copy.144
  30.9 0.1 fusion.46
  31.0 0.1 copy.147
  31.1 0.1 copy.145
  31.4 2.9 %fusion.53 = (bf16[1,2,1024,576]{2,3,1,0:T(8,128)(2,1)S(1)}, bf16[1,2,1024,576]{2,3,1,0:T(8,128)(2,1)S(1)}) fusion(bf16[2,2,1024,576]{2,3,1,0:T(8,128)(2,1)} %param.11), kind=kLoop, calls=%fused_computation.77 | loop fusion | bytes 9437184 | tf_op jit(solution)/shard_map/slice | solution.py:80
  34.4 0.5 fusion.57
  34.9 0.3 fusion.12
  35.1 0.7 fusion.9
  35.9 0.2 fusion.10
  36.2 2.2 %convolution_bitcast_fusion.1 = f32[2304,8]{1,0:T(8,128)} fusion(bf16[8,576]{1,0:T(8,128)(2,1)S(1)} %reshape_reshape.6, bf16[576,2304]{1,0:T(8,128)(2,1)S(1)} %copy-done), kind=kOutput, calls=%fused_computation.2 | convolution fusion | flops 21233664 | bytes 2737152
  38.5 0.1 copy.150
  38.6 50.1 %all-gather.1 = f32[256,9,4]{1,2,0:T(4,128)S(1)} all-gather(f32[4,9,4]{1,2,0:T(4,128)S(1)} %copy.150), channel_id=3, replica_groups=mesh['seq'=64,'tp'=4] {'seq'}, dimensions={0}, use_global_device_ids=true | all-gather | bytes 37440 | tf_op jit(solution)/shard_map/all_gather | solution.py:94
  88.7 0.8 copy-done.1
  89.5 0.1 reduce_max.58
  89.6 1.2 subtract_exponential_fusion
  91.0 0.2 fusion.26
  91.1 0.2 copy.154
  91.3 0.1 fusion.28
  91.5 0.1 fusion.38
  91.6 3.0 %copy.151 = f32[64,4,9,4]{3,2,1,0:T(8,128)} copy(f32[64,4,9,4]{2,3,1,0:T(4,128)S(1)} %subtract_exponential_fusion) | data formatting | bytes 73728 | tf_op jit(solution)/shard_map/exp | solution.py:99
  94.6 0.2 copy.159
  94.9 0.5 broadcast.55
  95.4 0.8 reduce
  96.2 1.5 %reshape.154 = f32[64,1,4,4,9]{4,3,2,1,0:T(4,128)} reshape(f32[64,144]{1,0:T(8,128)S(1)} %reduce) | data formatting | bytes 73728
  97.8 1.2 fusion.11
  99.0 0.1 copy.157
  99.1 0.1 copy.161
  99.2 0.1 copy.165
  99.4 6.3 %multiply_reduce_fusion = f32[4,9,4,64]{3,2,1,0:T(4,128)S(1)} fusion(f32[64,4,9,4,64]{4,3,2,1,0:T(4,128)} %bitcast.98, f32[64,4,9,4]{3,2,1,0:T(8,128)} %copy.151), kind=kLoop, calls=%fused_computation | loop fusion | flops 1170432 | bytes 2433024 | tf_op jit(solution)/shard_map/reduce_sum | solution.py:103
  105.6 0.2 fusion.5
  105.9 0.1 reshape_reshape.7
  106.0 2.2 %convolution_bitcast_fusion = f32[2304,16]{1,0:T(8,128)} fusion(bf16[16,576]{1,0:T(8,128)(2,1)S(1)} %reshape_reshape.7, bf16[576,2304]{1,0:T(8,128)(2,1)S(1)} %copy-done), kind=kOutput, calls=%fused_computation.1 | convolution fusion | flops 42467328 | bytes 2820096
  108.2 1.0 copy.168
  109.3 0.6 reshape.143
  109.9 24.3 %reduce-scatter.9.cloned.1.call-done = f32[576,16]{1,0:T(8,128)} async-done(((f32[2304,16]{1,0:T(8,128)}), f32[576,16]{1,0:T(8,128)}) %reduce-scatter.9.cloned.1.call-update) | async-done | bytes 36880
  134.2 1.1 copy.170
  135.3 0.6 reshape.146
  (42 shorter events, 1.2 us)
Async XLA Ops:
  8.0 28.2 %copy-start = (bf16[576,2304]{1,0:T(8,128)(2,1)S(1)}, bf16[576,2304]{1,0:T(8,128)(2,1)}, u32[]{:S(2)}) copy-start(bf16[576,2304]{1,0:T(8,128)(2,1)} %param.19) | copy-start | bytes 7962628
  8.0 91.3 %all-gather.4.cloned.1.call-start = ((), (), s32[]{:S(2)}) async-start(), calls=%async_computation.3 | async-start | bytes 4792320 | tf_op jit(solution)/shard_map/all_gather | solution.py:96
  8.9 3.2 %copy-start.4 = (bf16[4,4,576]{2,1,0:T(4,128)(2,1)S(1)}, bf16[4,4,576]{2,1,0:T(4,128)(2,1)}, u32[]{:S(2)}) copy-start(bf16[4,4,576]{2,1,0:T(4,128)(2,1)} %param.14) | copy-start | bytes 55300
  8.9 3.3 %copy-start.7 = (s32[4]{0:T(128)S(1)}, s32[4]{0:T(128)}, u32[]{:S(2)}) copy-start(s32[4]{0:T(128)} %param.17) | copy-start | bytes 52
  12.1 18.1 %copy-start.5 = (bf16[2,4,576]{2,1,0:T(4,128)(2,1)S(1)}, bf16[2,4,576]{2,1,0:T(4,128)(2,1)}, u32[]{:S(2)}) copy-start(bf16[2,4,576]{2,1,0:T(4,128)(2,1)} %param.10) | copy-start | bytes 27652
  12.1 18.1 %copy-start.3 = (bf16[2,2,4,576]{3,2,1,0:T(4,128)(2,1)S(1)}, bf16[2,2,4,576]{3,2,1,0:T(4,128)(2,1)}, u32[]{:S(2)}) copy-start(bf16[2,2,4,576]{3,2,1,0:T(4,128)(2,1)} %param.12) | copy-start | bytes 55300
  12.3 19.0 %copy-start.6 = (s32[2]{0:T(128)S(1)}, s32[2]{0:T(128)}, u32[]{:S(2)}) copy-start(s32[2]{0:T(128)} %param.13) | copy-start | bytes 28
  18.0 76.9 %all-to-all-start = ((f32[64,1,144]{2,1,0:T(1,128)}), f32[64,1,144]{2,1,0:T(1,128)S(1)}, u32[]{:S(2)}, u32[]{:S(2)}) async-start(f32[64,1,144]{2,1,0:T(1,128)} %reshape.153), calls=%async_computation | async-start | bytes 131072 | tf_op jit(solution)/shard_map/all_to_all | solution.py:13
  30.1 78.1 %reduce-scatter.7.cloned.1.call-start = ((), (), s32[]{:S(2)}) async-start(), calls=%async_computation.4 | async-start | bytes 1474560
  38.4 52.4 %copy-start.2 = (bf16[2,4,4,576]{3,2,1,0:T(4,128)(2,1)S(1)}, bf16[2,4,4,576]{3,2,1,0:T(4,128)(2,1)}, u32[]{:S(2)}) copy-start(bf16[2,4,4,576]{3,2,1,0:T(4,128)(2,1)} %param.16) | copy-start | bytes 110596
  38.4 95.8 %reduce-scatter.9.cloned.1.call-start = ((), (), s32[]{:S(2)}) async-start(), calls=%async_computation.5 | async-start | bytes 1474560
  88.7 0.8 copy-start.1
Sparse Core Ops, SparseCore 0:
  16.5 81.0 all-gather.3
Sparse Core Ops, SparseCore 1:
  38.5 27.6 reduce-scatter.6
  108.3 25.9 reduce-scatter.8
